TPU v7x, 256 devices: a whole 4x4x8 slice. The times are simulated.
256 devices in a mesh: dp: 32 (over y, x, core), filter: 8 (over z).
Axes of the slice: x: 4, y: 4, z: 8, core: 2. Of those that a mesh axis runs over, the one named last changes fastest.
Arguments:
- inputs: bfloat16 [32, 48, 24, 1024], P('dp', None, None, 'filter'), may hold values from -6 to 6
- kernel: bfloat16 [3, 3, 1024, 1024], P(None, None, 'filter'), may hold values from -0.0625 to 0.0625
- cotangent: bfloat16 [32, 48, 24, 1024], P('dp', 'filter'), may hold values from -6 to 6
Outputs:
- outputs: bfloat16 [32, 48, 24, 1024], P('dp', 'filter')
- input_grad: bfloat16 [32, 48, 24, 1024], P('dp', None, None, 'filter')
- kernel_grad: float32 [1024, 3, 3, 1024], P('dp', None, None, 'filter')
All inputs are finite; a program needn't handle non-finite values.
Results may differ from a plain program's by a relative error of at most 0.001.
Values may be sent and summed in bfloat16 or wider, within the bound.
No kernel may reach another device: no remote copies, remote signals or barrier semaphores. Data moves between devices by JAX's collectives and lax.ppermute only.
A program may use at most 128 MiB of HBM per device.

v0:
```python
import jax
import jax.numpy as jnp
from jax import lax
from jax.sharding import PartitionSpec as P


def conv_rows(xpad, weights, count, width):
    total = jnp.zeros((count, width, weights.shape[3]), jnp.float32)
    for a in range(3):
        for b in range(3):
            total = total + jnp.einsum(
                "hwi,io->hwo",
                xpad[a : a + count, b : b + width],
                weights[a, b],
                preferred_element_type=jnp.float32,
            )
    return total


def on_device(inputs, kernel, cotangent):
    sample = inputs[0]
    height = sample.shape[0]
    width = sample.shape[1]
    local_in = sample.shape[2]
    channels = kernel.shape[3]
    groups = lax.axis_size("filter")
    my_rows = height // groups
    xpad = jnp.pad(sample, ((1, 1), (1, 1), (0, 0)))
    summed = lax.psum_scatter(
        conv_rows(xpad, kernel, my_rows * lax.axis_size("filter"), width),
        "filter",
        scatter_dimension=0,
        tiled=True,
    )
    outputs = summed.astype(jnp.bfloat16)[None]
    start = jnp.int32(0)
    back_pad = jnp.zeros((height + 2, width + 2, local_in), jnp.float32)
    grad_rows = lax.all_gather(cotangent, "filter", axis=1, tiled=True)[0]
    count = grad_rows.shape[0]
    taps = []
    for a in range(3):
        for b in range(3):
            contrib = jnp.einsum(
                "hwo,io->hwi", grad_rows, kernel[a, b], preferred_element_type=jnp.float32
            )
            region = lax.dynamic_slice(back_pad, (start + a, b, 0), (count, width, local_in))
            back_pad = lax.dynamic_update_slice(back_pad, region + contrib, (start + a, b, 0))
            taps.append(
                jnp.einsum(
                    "hwi,hwo->oi",
                    xpad[a : a + count, b : b + width],
                    grad_rows,
                    preferred_element_type=jnp.float32,
                )
            )
    grads = jnp.stack(taps, 1).reshape(channels, 3, 3, local_in)
    back_pad, grads = (back_pad, grads)
    input_grad = back_pad[1:-1, 1:-1].astype(jnp.bfloat16)[None]
    samples = lax.axis_size("dp")
    scale = 1.0 / jnp.sqrt(jnp.float32(samples * height * width))
    whole = lax.psum(grads, "dp")
    share = channels // samples
    mine = lax.dynamic_slice_in_dim(whole, lax.axis_index("dp") * share, share, 0)
    return (outputs, input_grad, mine * scale)


def solution(mesh):
    return jax.shard_map(
        on_device,
        mesh=mesh,
        in_specs=(
            P("dp", None, None, "filter"),
            P(None, None, "filter", None),
            P("dp", "filter", None, None),
        ),
        out_specs=(
            P("dp", "filter", None, None),
            P("dp", None, None, "filter"),
            P("dp", None, None, "filter"),
        ),
        check_vma=False,
    )
```

profile of v0, /device:TPU:1, one launch (start us, length us, event | category | flops | bytes accessed | tf_op | source)
XLA Modules:
  0.0 268.3 jit_solution(1624768555959365311)
XLA Ops:
  8.0 4.1 %fusion.124 = f32[48,24,1024]{2,1,0:T(8,128)} fusion(bf16[3,3,128,1024]{3,2,1,0:T(8,128)(2,1)} %param.4, bf16[48,24,128]{2,1,0:T(8,128)(2,1)} %bitcast.236), kind=kOutput, calls=%fused_computation.79 | convolution fusion | flops 301989888 | bytes 5275648 | tf_op jit(solution)/shard_map/hwi,io->hwo/dot_general | solution.py:11
  12.0 3.8 %fusion.127 = f32[48,24,1024]{2,1,0:T(8,128)} fusion(bf16[3,3,128,1024]{3,2,1,0:T(8,128)(2,1)} %param.4, bf16[48,24,128]{2,1,0:T(8,128)(2,1)S(1)} %bitcast.237), kind=kOutput, calls=%fused_computation.82 | convolution fusion | flops 301989888 | bytes 5275648 | tf_op jit(solution)/shard_map/hwi,io->hwo/dot_general | solution.py:11
  15.8 3.9 %fusion.130 = f32[48,24,1024]{2,1,0:T(8,128)} fusion(bf16[3,3,128,1024]{3,2,1,0:T(8,128)(2,1)} %param.4, bf16[48,24,128]{2,1,0:T(8,128)(2,1)S(1)} %bitcast.238), kind=kOutput, calls=%fused_computation.85 | convolution fusion | flops 301989888 | bytes 5275648 | tf_op jit(solution)/shard_map/hwi,io->hwo/dot_general | solution.py:11
  19.8 3.9 %fusion.136 = f32[48,24,1024]{2,1,0:T(8,128)} fusion(bf16[3,3,128,1024]{3,2,1,0:T(8,128)(2,1)} %param.4, bf16[48,24,128]{2,1,0:T(8,128)(2,1)S(1)} %bitcast.239), kind=kOutput, calls=%fused_computation.91 | convolution fusion | flops 301989888 | bytes 5275648 | tf_op jit(solution)/shard_map/hwi,io->hwo/dot_general | solution.py:11
  23.6 3.9 %fusion.139 = f32[48,24,1024]{2,1,0:T(8,128)} fusion(bf16[3,3,128,1024]{3,2,1,0:T(8,128)(2,1)} %param.4, bf16[48,24,128]{2,1,0:T(8,128)(2,1)S(1)} %bitcast.240), kind=kOutput, calls=%fused_computation.94 | convolution fusion | flops 301989888 | bytes 5275648 | tf_op jit(solution)/shard_map/hwi,io->hwo/dot_general | solution.py:11
  27.5 24.7 %all-gather.2.cloned.1.call-done = bf16[1,48,24,1024]{3,2,0,1:T(8,128)(2,1)} async-done(((bf16[1,6,24,1024]{3,2,0,1:T(8,128)(2,1)}), bf16[1,48,24,1024]{3,2,0,1:T(8,128)(2,1)}) %all-gather.2.cloned.1.call-update) | async-done | bytes 2359312 | tf_op jit(solution)/shard_map/all_gather | solution.py:38
  52.3 3.2 %fusion.69 = f32[1024,9,128]{0,2,1:T(8,128)} fusion(bf16[1,48,24,1024]{3,2,0,1:T(8,128)(2,1)} %all-gather.2.cloned.1.call-done, bf16[48,24,128]{2,1,0:T(8,128)(2,1)S(1)} %bitcast.241), kind=kOutput, calls=%fused_computation.48 | convolution fusion | flops 301989888 | bytes 3178496 | tf_op jit(solution)/shard_map/hwi,hwo->oi/dot_general | solution.py:49
  66.3 6.0 %copy.46 = f32[1024,3,3,128]{3,0,2,1:T(8,128)} copy(f32[1024,3,3,128]{0,3,2,1:T(8,128)} %bitcast.58) | data formatting | bytes 9437184 | tf_op jit(solution)/shard_map/reshape | solution.py:56
  72.4 4.2 %fusion.145 = f32[48,24,1024]{2,1,0:T(8,128)} fusion(bf16[3,3,128,1024]{3,2,1,0:T(8,128)(2,1)} %param.4, bf16[48,24,128]{2,1,0:T(8,128)(2,1)S(1)} %bitcast.249), kind=kOutput, calls=%fused_computation.100 | convolution fusion | flops 301989888 | bytes 5275648 | tf_op jit(solution)/shard_map/hwi,io->hwo/dot_general | solution.py:11
  76.6 4.0 %fusion.142 = f32[48,24,1024]{2,1,0:T(8,128)} fusion(bf16[3,3,128,1024]{3,2,1,0:T(8,128)(2,1)} %param.4, bf16[48,24,128]{2,1,0:T(8,128)(2,1)S(1)} %bitcast.250), kind=kOutput, calls=%fused_computation.97 | convolution fusion | flops 301989888 | bytes 5275648 | tf_op jit(solution)/shard_map/hwi,io->hwo/dot_general | solution.py:11
  80.6 3.9 %fusion.133 = f32[48,24,1024]{2,1,0:T(8,128)} fusion(bf16[3,3,128,1024]{3,2,1,0:T(8,128)(2,1)} %param.4, bf16[1,48,24,128]{3,2,1,0:T(8,128)(2,1)S(1)} %copy-done.1), kind=kOutput, calls=%fused_computation.88 | convolution fusion | flops 301989888 | bytes 5275648 | tf_op jit(solution)/shard_map/hwi,io->hwo/dot_general | solution.py:11
  84.6 13.1 %add_add_fusion = f32[48,24,1024]{2,1,0:T(8,128)} fusion(f32[48,24,1024]{2,1,0:T(8,128)S(1)} %bitcast.253, f32[48,24,1024]{2,1,0:T(8,128)S(1)} %bitcast.255, f32[48,24,1024]{2,1,0:T(8,128)} %fusion.130, f32[48,24,1024]{2,1,0:T(8,128)} %fusion.133, f32[48,24,1024]{2,1,0:T(8,128)} %fusion.136, f32[48,24,1024]{2,1,0:T(8,128)} %fusion.139, ...), kind=kOutput, calls=%fused_computation | convolution fusion | flops 311427072 | bytes 43024384 | tf_op jit(solution)/shard_map/hwi,io->hwo/dot_general | solution.py:11
  99.6 2.6 fusion.36
  102.1 6.3 %dynamic_update_slice.28 = f32[50,26,128]{2,1,0:T(8,128)S(1)} dynamic-update-slice(f32[50,26,128]{2,1,0:T(8,128)S(1)} %dynamic_update_slice.27, f32[48,24,128]{2,1,0:T(8,128)} %fusion.36, s32[]{:T(128)} %constant.5.clone.1, s32[]{:T(128)} %constant.6.clone.1, s32[]{:T(128)} %constant.5.clone.1) | dynamic-update-slice | bytes 1179652 | tf_op jit(solution)/shard_map/dynamic_update_slice | solution.py:47
  108.5 2.6 fusion.39
  111.0 6.3 %dynamic_update_slice.29 = f32[50,26,128]{2,1,0:T(8,128)S(1)} dynamic-update-slice(f32[50,26,128]{2,1,0:T(8,128)S(1)} %dynamic_update_slice.28, f32[48,24,128]{2,1,0:T(8,128)} %fusion.39, s32[]{:T(128)} %constant.5.clone.1, s32[]{:T(128)} %constant.7.clone.1, s32[]{:T(128)} %constant.5.clone.1) | dynamic-update-slice | bytes 1179652 | tf_op jit(solution)/shard_map/dynamic_update_slice | solution.py:47
  121.8 6.3 %dynamic_update_slice.31 = f32[50,26,128]{2,1,0:T(8,128)S(1)} dynamic-update-slice(f32[50,26,128]{2,1,0:T(8,128)S(1)} %fusion.45, f32[48,24,128]{2,1,0:T(8,128)} %fusion.48, s32[]{:T(128)} %constant.6.clone.1, s32[]{:T(128)} %constant.6.clone.1, s32[]{:T(128)} %constant.5.clone.1) | dynamic-update-slice | bytes 1179652 | tf_op jit(solution)/shard_map/dynamic_update_slice | solution.py:47
  128.1 2.6 fusion.51
  130.6 6.3 %dynamic_update_slice.32 = f32[50,26,128]{2,1,0:T(8,128)S(1)} dynamic-update-slice(f32[50,26,128]{2,1,0:T(8,128)S(1)} %dynamic_update_slice.31, f32[48,24,128]{2,1,0:T(8,128)} %fusion.51, s32[]{:T(128)} %constant.6.clone.1, s32[]{:T(128)} %constant.7.clone.1, s32[]{:T(128)} %constant.5.clone.1) | dynamic-update-slice | bytes 1179652 | tf_op jit(solution)/shard_map/dynamic_update_slice | solution.py:47
  141.3 6.2 %dynamic_update_slice.34 = f32[50,26,128]{2,1,0:T(8,128)S(1)} dynamic-update-slice(f32[50,26,128]{2,1,0:T(8,128)S(1)} %fusion.57, f32[48,24,128]{2,1,0:T(8,128)} %fusion.60, s32[]{:T(128)} %constant.7.clone.1, s32[]{:T(128)} %constant.6.clone.1, s32[]{:T(128)} %constant.5.clone.1) | dynamic-update-slice | bytes 1179652 | tf_op jit(solution)/shard_map/dynamic_update_slice | solution.py:47
  147.6 2.6 fusion.63
  150.1 6.2 %dynamic_update_slice.35 = f32[50,26,128]{2,1,0:T(8,128)S(1)} dynamic-update-slice(f32[50,26,128]{2,1,0:T(8,128)S(1)} %dynamic_update_slice.34, f32[48,24,128]{2,1,0:T(8,128)} %fusion.63, s32[]{:T(128)} %constant.7.clone.1, s32[]{:T(128)} %constant.7.clone.1, s32[]{:T(128)} %constant.5.clone.1) | dynamic-update-slice | bytes 1179652 | tf_op jit(solution)/shard_map/dynamic_update_slice | solution.py:47
  157.1 40.0 %all-reduce.4.cloned.1.call-done = f32[1024,3,3,128]{3,0,2,1:T(8,128)} async-done(((f32[1024,3,3,128]{3,0,2,1:T(8,128)}), f32[1024,3,3,128]{3,0,2,1:T(8,128)}) %all-reduce.4.cloned.1.call-update) | async-done | bytes 4718608 | tf_op jit(solution)/shard_map/psum | solution.py:61
  198.8 61.2 %reduce-scatter.2.cloned.1.call-done = f32[6,24,1024]{2,1,0:T(8,128)} async-done(((f32[48,24,1024]{2,1,0:T(8,128)}), f32[6,24,1024]{2,1,0:T(8,128)}) %reduce-scatter.2.cloned.1.call-update) | async-done | bytes 589840 | tf_op jit(solution)/shard_map/reduce_scatter | solution.py:29
  (37 shorter events, 26.6 us)
Async XLA Ops:
  7.2 45.1 %all-gather.2.cloned.1.call-start = ((), (), s32[]{:S(2)}) async-start(), calls=%async_computation.2 | async-start | bytes 2654208 | tf_op jit(solution)/shard_map/all_gather | solution.py:38
  7.9 189.3 %all-reduce.4.cloned.1.call-start = ((), (), s32[]{:S(2)}) async-start(), calls=%async_computation.3 | async-start | bytes 9437184 | tf_op jit(solution)/shard_map/psum | solution.py:61
  7.9 4.1 %copy-start.1 = (bf16[1,48,24,128]{3,2,1,0:T(8,128)(2,1)S(1)}, bf16[1,48,24,128]{3,2,1,0:T(8,128)(2,1)}, u32[]{:S(2)}) copy-start(bf16[1,48,24,128]{3,2,1,0:T(8,128)(2,1)} %param.3) | copy-start | bytes 884740
  52.3 3.2 %copy-start = (bf16[1,48,24,1024]{3,2,0,1:T(8,128)(2,1)S(1)}, bf16[1,48,24,1024]{3,2,0,1:T(8,128)(2,1)}, u32[]{:S(2)}) copy-start(bf16[1,48,24,1024]{3,2,0,1:T(8,128)(2,1)} %all-gather.2.cloned.1.call-done) | copy-start | bytes 7077892
  72.3 187.6 %reduce-scatter.2.cloned.1.call-start = ((), (), s32[]{:S(2)}) async-start(), calls=%async_computation.1 | async-start | bytes 5308416 | tf_op jit(solution)/shard_map/reduce_scatter | solution.py:29
  72.4 12.2 %slice-start = ((s8[4718592]{0:T(1024)(128)(4,1)}), s8[4194304]{0:T(1024)(128)(4,1)S(1)}, s32[]{:S(2)}) async-start(s8[4718592]{0:T(1024)(128)(4,1)} %bitcast.252), calls=%async_computation.4 | async-start | bytes 8388608
  72.4 12.2 %slice-start.2 = ((s8[4718592]{0:T(1024)(128)(4,1)}), s8[4194304]{0:T(1024)(128)(4,1)S(1)}, s32[]{:S(2)}) async-start(s8[4718592]{0:T(1024)(128)(4,1)} %bitcast.254), calls=%async_computation.6 | async-start | bytes 8388608
  76.6 8.0 %slice-start.1 = ((s8[4718592]{0:T(1024)(128)(4,1)}), s8[524288]{0:T(1024)(128)(4,1)S(1)}, s32[]{:S(2)}) async-start(s8[4718592]{0:T(1024)(128)(4,1)} %bitcast.252), calls=%async_computation.5 | async-start | bytes 1048576
  76.6 8.0 %slice-start.3 = ((s8[4718592]{0:T(1024)(128)(4,1)}), s8[524288]{0:T(1024)(128)(4,1)S(1)}, s32[]{:S(2)}) async-start(s8[4718592]{0:T(1024)(128)(4,1)} %bitcast.254), calls=%async_computation.7 | async-start | bytes 1048576
Sparse Core Ops, SparseCore 0:
  9.8 42.4 all-gather.1
  72.5 124.6 all-reduce.3
  199.9 59.9 reduce-scatter.1
where the time goes:
time: 270 us; the launch traced here: 268 us
  waiting for transfers between devices  127 us (47%)
  matrix products  79.7 us (30%)
  local copies, waits for them, and re-layouts  44.6 us (17%)
  between operations  13.9 us (5%)
  other arithmetic  3.4 us (1%)
    reduce_scatter x1, waiting for transfers between devices, on_device(): lax.psum_scatter(conv_rows(xpad, kernel, my_rows * lax.axis_size('filter'...  61.2 us
    dot_general x9, matrix products, conv_rows(): jnp.einsum('hwi,io->hwo', xpad[a:a + count, b:b + width], weights[a, b],...  44.8 us
    psum x1, waiting for transfers between devices, on_device(): whole = lax.psum(grads, 'dp')  40 us
    dynamic_update_slice x7, local copies, waits for them, and re-layouts, on_device(): lax.dynamic_update_slice(back_pad, region + contrib, (start + a, b, 0))  37.7 us
    all_gather x1, waiting for transfers between devices, on_device(): grad_rows = lax.all_gather(cotangent, 'filter', axis=1, tiled=True)[0]  24.7 us
    dot_general x9, matrix products, on_device(): jnp.einsum('hwo,io->hwi', grad_rows, kernel[a, b], preferred_element_type...  20.9 us
    dot_general x9, matrix products, on_device(): jnp.einsum('hwi,hwo->oi', xpad[a:a + count, b:b + width], grad_rows, pref...  14 us
    reshape x1, local copies, waits for them, and re-layouts, on_device(): grads = jnp.stack(taps, 1).reshape(channels, 3, 3, local_in)  6.04 us
  transfers between devices with their start and end apart: 3, of which 3 were waited for; matrix products, arithmetic and copies ran while one was open for 39% of the time, Pallas kernels for 0%

commit v1 on v0

--- a/solution.py
+++ b/solution.py
@@ -58,7 +58,9 @@
     input_grad = back_pad[1:-1, 1:-1].astype(jnp.bfloat16)[None]
     samples = lax.axis_size("dp")
     scale = 1.0 / jnp.sqrt(jnp.float32(samples * height * width))
-    whole = lax.psum(grads, "dp")
+    whole = grads
+    for hop in (1, 2, 4, 8, 16):
+        whole = whole + lax.ppermute(whole, "dp", [(dev, dev ^ hop) for dev in range(32)])
     share = channels // samples
     mine = lax.dynamic_slice_in_dim(whole, lax.axis_index("dp") * share, share, 0)
     return (outputs, input_grad, mine * scale)

time: 270 us -> 519 us (1.92)
  waiting for transfers between devices: 127 us -> 362 us
  matrix products: 79.7 us -> 66.8 us
  other arithmetic: 3.4 us -> 16 us
  starting transfers between devices: 0.12 us -> 11.8 us
    ppermute x0 -> x5, waiting for transfers between devices: none -> 317 us  [on_device(): lax.ppermute(whole, 'dp', [(dev, dev ^ hop) for dev in range(32)])]
    reduce_scatter x1, waiting for transfers between devices: 61.2 us -> 0.01 us  [on_device(): lax.psum_scatter(conv_rows(xpad, kernel, my_rows * lax.axis_size('filter'...]
    psum x1 -> x0, waiting for transfers between devices: 40 us -> none  [on_device(): whole = lax.psum(grads, 'dp')]
    all_gather x1, waiting for transfers between devices: 24.7 us -> 44.3 us  [on_device(): grad_rows = lax.all_gather(cotangent, 'filter', axis=1, tiled=True)[0]]
    dot_general x9, matrix products: 44.8 us -> 31.8 us  [conv_rows(): jnp.einsum('hwi,io->hwo', xpad[a:a + count, b:b + width], weights[a, b],...]
    add x0 -> x4, other arithmetic: none -> 12.6 us  [on_device(): whole + lax.ppermute(whole, 'dp', [(dev, dev ^ hop) for dev in range(32)])]
    ppermute x0 -> x5, starting transfers between devices: none -> 11.7 us  [on_device(): lax.ppermute(whole, 'dp', [(dev, dev ^ hop) for dev in range(32)])]
  transfers between devices with their start and end apart: 3 -> 7, of which waited for: 3 -> 6; matrix products, arithmetic and copies ran while one was open for 39% -> 19% of each run, Pallas kernels for 0% -> 0%
where the time goes in v1:
time: 519 us; the launch traced here: 515 us
  waiting for transfers between devices  362 us (70%)
  matrix products  66.8 us (13%)
  local copies, waits for them, and re-layouts  44.6 us (9%)
  other arithmetic  16 us (3%)
  between operations  14.2 us (3%)
  starting transfers between devices  11.8 us (2%)
    ppermute x5, waiting for transfers between devices, on_device(): lax.ppermute(whole, 'dp', [(dev, dev ^ hop) for dev in range(32)])  317 us
    all_gather x1, waiting for transfers between devices, on_device(): grad_rows = lax.all_gather(cotangent, 'filter', axis=1, tiled=True)[0]  44.3 us
    dynamic_update_slice x7, local copies, waits for them, and re-layouts, on_device(): lax.dynamic_update_slice(back_pad, region + contrib, (start + a, b, 0))  37.7 us
    dot_general x9, matrix products, conv_rows(): jnp.einsum('hwi,io->hwo', xpad[a:a + count, b:b + width], weights[a, b],...  31.8 us
    dot_general x9, matrix products, on_device(): jnp.einsum('hwo,io->hwi', grad_rows, kernel[a, b], preferred_element_type...  21 us
    dot_general x9, matrix products, on_device(): jnp.einsum('hwi,hwo->oi', xpad[a:a + count, b:b + width], grad_rows, pref...  14 us
    add x4, other arithmetic, on_device(): whole + lax.ppermute(whole, 'dp', [(dev, dev ^ hop) for dev in range(32)])  12.6 us
    ppermute x5, starting transfers between devices, on_device(): lax.ppermute(whole, 'dp', [(dev, dev ^ hop) for dev in range(32)])  11.7 us
  transfers between devices with their start and end apart: 7, of which 6 were waited for; matrix products, arithmetic and copies ran while one was open for 19% of the time, Pallas kernels for 0%

profile of v1, /device:TPU:1, one launch (start us, length us, event | category | flops | bytes accessed | tf_op | source)
XLA Modules:
  0.0 515.2 jit_solution(9559041117039875025)
XLA Ops:
  8.0 44.3 %all-gather.2.cloned.1.call-done = bf16[1,48,24,1024]{3,2,0,1:T(8,128)(2,1)} async-done(((bf16[1,6,24,1024]{3,2,0,1:T(8,128)(2,1)}), bf16[1,48,24,1024]{3,2,0,1:T(8,128)(2,1)}) %all-gather.2.cloned.1.call-update) | async-done | bytes 2359312 | tf_op jit(solution)/shard_map/all_gather | solution.py:38
  52.3 3.2 fusion.69
  66.3 6.1 %copy.48 = f32[1024,3,3,128]{3,0,2,1:T(8,128)} copy(f32[1024,3,3,128]{0,3,2,1:T(8,128)} %bitcast.58) | data formatting | bytes 9437184 | tf_op jit(solution)/shard_map/reshape | solution.py:56
  72.4 3.6 collective-permute-start
  76.0 7.7 %collective-permute-done = f32[1024,3,3,128]{3,0,2,1:T(8,128)S(1)} collective-permute-done((f32[1024,3,3,128]{3,0,2,1:T(8,128)}, f32[1024,3,3,128]{3,0,2,1:T(8,128)S(1)}, u32[]{:S(2)}, u32[]{:S(2)}) %collective-permute-start) | collective-permute-done | bytes 4718624 | tf_op jit(solution)/shard_map/ppermute | solution.py:63
  83.8 3.1 add.88
  88.1 101.8 %collective-permute-done.1 = f32[1024,3,3,128]{3,0,2,1:T(8,128)S(1)} collective-permute-done((f32[1024,3,3,128]{3,0,2,1:T(8,128)S(1)}, f32[1024,3,3,128]{3,0,2,1:T(8,128)S(1)}, u32[]{:S(2)}, u32[]{:S(2)}) %collective-permute-start.1) | collective-permute-done | bytes 4718624 | tf_op jit(solution)/shard_map/ppermute | solution.py:63
  196.9 3.0 fusion.130
  199.9 2.9 fusion.136
  202.7 3.0 fusion.139
  205.7 3.0 fusion.145
  208.7 2.9 fusion.142
  211.6 3.0 fusion.133
  214.6 12.5 %add_add_fusion = f32[48,24,1024]{2,1,0:T(8,128)} fusion(f32[48,24,1024]{2,1,0:T(8,128)S(1)} %fusion.124, f32[48,24,1024]{2,1,0:T(8,128)S(1)} %fusion.127, f32[48,24,1024]{2,1,0:T(8,128)} %fusion.130, f32[48,24,1024]{2,1,0:T(8,128)} %fusion.133, f32[48,24,1024]{2,1,0:T(8,128)} %fusion.136, f32[48,24,1024]{2,1,0:T(8,128)} %fusion.139, ...), kind=kOutput, calls=%fused_computation | convolution fusion | flops 311427072 | bytes 43024384 | tf_op jit(solution)/shard_map/hwi,io->hwo/dot_general | solution.py:11
  227.1 69.4 %collective-permute-done.2 = f32[1024,3,3,128]{3,0,2,1:T(8,128)} collective-permute-done((f32[1024,3,3,128]{3,0,2,1:T(8,128)}, f32[1024,3,3,128]{3,0,2,1:T(8,128)}, u32[]{:S(2)}, u32[]{:S(2)}) %collective-permute-start.2) | collective-permute-done | bytes 4718624 | tf_op jit(solution)/shard_map/ppermute | solution.py:63
  296.5 4.3 add.90
  302.2 99.9 %collective-permute-done.3 = f32[1024,3,3,128]{3,0,2,1:T(8,128)S(1)} collective-permute-done((f32[1024,3,3,128]{3,0,2,1:T(8,128)S(1)}, f32[1024,3,3,128]{3,0,2,1:T(8,128)S(1)}, u32[]{:S(2)}, u32[]{:S(2)}) %collective-permute-start.3) | collective-permute-done | bytes 4718624 | tf_op jit(solution)/shard_map/ppermute | solution.py:63
  411.8 6.3 %dynamic_update_slice.28 = f32[50,26,128]{2,1,0:T(8,128)S(1)} dynamic-update-slice(f32[50,26,128]{2,1,0:T(8,128)S(1)} %dynamic_update_slice.27, f32[48,24,128]{2,1,0:T(8,128)} %fusion.36, s32[]{:T(128)} %constant.5.clone.1, s32[]{:T(128)} %constant.6.clone.1, s32[]{:T(128)} %constant.5.clone.1) | dynamic-update-slice | bytes 1179652 | tf_op jit(solution)/shard_map/dynamic_update_slice | solution.py:47
  420.7 6.3 %dynamic_update_slice.29 = f32[50,26,128]{2,1,0:T(8,128)S(1)} dynamic-update-slice(f32[50,26,128]{2,1,0:T(8,128)S(1)} %dynamic_update_slice.28, f32[48,24,128]{2,1,0:T(8,128)} %fusion.39, s32[]{:T(128)} %constant.5.clone.1, s32[]{:T(128)} %constant.7.clone.1, s32[]{:T(128)} %constant.5.clone.1) | dynamic-update-slice | bytes 1179652 | tf_op jit(solution)/shard_map/dynamic_update_slice | solution.py:47
  431.5 6.3 %dynamic_update_slice.31 = f32[50,26,128]{2,1,0:T(8,128)S(1)} dynamic-update-slice(f32[50,26,128]{2,1,0:T(8,128)S(1)} %fusion.45, f32[48,24,128]{2,1,0:T(8,128)} %fusion.48, s32[]{:T(128)} %constant.6.clone.1, s32[]{:T(128)} %constant.6.clone.1, s32[]{:T(128)} %constant.5.clone.1) | dynamic-update-slice | bytes 1179652 | tf_op jit(solution)/shard_map/dynamic_update_slice | solution.py:47
  440.4 6.3 %dynamic_update_slice.32 = f32[50,26,128]{2,1,0:T(8,128)S(1)} dynamic-update-slice(f32[50,26,128]{2,1,0:T(8,128)S(1)} %dynamic_update_slice.31, f32[48,24,128]{2,1,0:T(8,128)} %fusion.51, s32[]{:T(128)} %constant.6.clone.1, s32[]{:T(128)} %constant.7.clone.1, s32[]{:T(128)} %constant.5.clone.1) | dynamic-update-slice | bytes 1179652 | tf_op jit(solution)/shard_map/dynamic_update_slice | solution.py:47
  451.1 6.2 %dynamic_update_slice.34 = f32[50,26,128]{2,1,0:T(8,128)S(1)} dynamic-update-slice(f32[50,26,128]{2,1,0:T(8,128)S(1)} %fusion.57, f32[48,24,128]{2,1,0:T(8,128)} %fusion.60, s32[]{:T(128)} %constant.7.clone.1, s32[]{:T(128)} %constant.6.clone.1, s32[]{:T(128)} %constant.5.clone.1) | dynamic-update-slice | bytes 1179652 | tf_op jit(solution)/shard_map/dynamic_update_slice | solution.py:47
  459.9 6.2 %dynamic_update_slice.35 = f32[50,26,128]{2,1,0:T(8,128)S(1)} dynamic-update-slice(f32[50,26,128]{2,1,0:T(8,128)S(1)} %dynamic_update_slice.34, f32[48,24,128]{2,1,0:T(8,128)} %fusion.63, s32[]{:T(128)} %constant.7.clone.1, s32[]{:T(128)} %constant.7.clone.1, s32[]{:T(128)} %constant.5.clone.1) | dynamic-update-slice | bytes 1179652 | tf_op jit(solution)/shard_map/dynamic_update_slice | solution.py:47
  468.7 38.0 %collective-permute-done.4 = f32[1024,3,3,128]{3,0,2,1:T(8,128)} collective-permute-done((f32[1024,3,3,128]{3,0,2,1:T(8,128)}, f32[1024,3,3,128]{3,0,2,1:T(8,128)}, u32[]{:S(2)}, u32[]{:S(2)}) %collective-permute-start.4) | collective-permute-done | bytes 4718624 | tf_op jit(solution)/shard_map/ppermute | solution.py:63
  (40 shorter events, 51.8 us)
Async XLA Ops:
  7.2 48.3 %copy-start.1 = (bf16[1,48,24,128]{3,2,1,0:T(8,128)(2,1)S(1)}, bf16[1,48,24,128]{3,2,1,0:T(8,128)(2,1)}, u32[]{:S(2)}) copy-start(bf16[1,48,24,128]{3,2,1,0:T(8,128)(2,1)} %param.3) | copy-start | bytes 884740
  7.2 45.1 %all-gather.2.cloned.1.call-start = ((), (), s32[]{:S(2)}) async-start(), calls=%async_computation.2 | async-start | bytes 2654208 | tf_op jit(solution)/shard_map/all_gather | solution.py:38
  7.9 459.0 %reduce-scatter.2.cloned.1.call-start = ((), (), s32[]{:S(2)}) async-start(), calls=%async_computation.1 | async-start | bytes 5308416 | tf_op jit(solution)/shard_map/reduce_scatter | solution.py:29
  52.3 3.2 copy-start
  72.4 11.4 %collective-permute-start = (f32[1024,3,3,128]{3,0,2,1:T(8,128)}, f32[1024,3,3,128]{3,0,2,1:T(8,128)S(1)}, u32[]{:S(2)}, u32[]{:S(2)}) collective-permute-start(f32[1024,3,3,128]{3,0,2,1:T(8,128)} %copy.48), channel_id=1, source_target_pairs={{0,8},{8,0},{16,24},{24,16},{32,40},{40,32},{48,56},{56,48},{64,72... | collective-permute-start | bytes 14155784 | tf_op jit(solution)/shard_map/ppermute | solution.py:63
  86.9 108.4 %copy-start.2 = (bf16[3,3,128,1024]{3,2,1,0:T(8,128)(2,1)S(1)}, bf16[3,3,128,1024]{3,2,1,0:T(8,128)(2,1)}, u32[]{:S(2)}) copy-start(bf16[3,3,128,1024]{3,2,1,0:T(8,128)(2,1)} %param.4) | copy-start | bytes 7077892
  86.9 103.1 %collective-permute-start.1 = (f32[1024,3,3,128]{3,0,2,1:T(8,128)S(1)}, f32[1024,3,3,128]{3,0,2,1:T(8,128)S(1)}, u32[]{:S(2)}, u32[]{:S(2)}) collective-permute-start(f32[1024,3,3,128]{3,0,2,1:T(8,128)S(1)} %add.88), channel_id=1, source_target_pairs={{0,16},{8,24},{16,0},{24,8},{32,48},{40,56},{48,32},{56,40},{64,80... | collective-permute-start | bytes 14155784 | tf_op jit(solution)/shard_map/ppermute | solution.py:63
  192.6 103.9 %collective-permute-start.2 = (f32[1024,3,3,128]{3,0,2,1:T(8,128)}, f32[1024,3,3,128]{3,0,2,1:T(8,128)}, u32[]{:S(2)}, u32[]{:S(2)}) collective-permute-start(f32[1024,3,3,128]{3,0,2,1:T(8,128)} %add.89), channel_id=1, source_target_pairs={{0,32},{8,40},{16,48},{24,56},{32,0},{40,8},{48,16},{56,24},{64,96... | collective-permute-start | bytes 14155784 | tf_op jit(solution)/shard_map/ppermute | solution.py:63
  300.8 101.3 %collective-permute-start.3 = (f32[1024,3,3,128]{3,0,2,1:T(8,128)S(1)}, f32[1024,3,3,128]{3,0,2,1:T(8,128)S(1)}, u32[]{:S(2)}, u32[]{:S(2)}) collective-permute-start(f32[1024,3,3,128]{3,0,2,1:T(8,128)S(1)} %add.90), channel_id=1, source_target_pairs={{0,64},{8,72},{16,80},{24,88},{32,96},{40,104},{48,112},{56,120},{... | collective-permute-start | bytes 14155784 | tf_op jit(solution)/shard_map/ppermute | solution.py:63
  404.7 102.1 %collective-permute-start.4 = (f32[1024,3,3,128]{3,0,2,1:T(8,128)}, f32[1024,3,3,128]{3,0,2,1:T(8,128)}, u32[]{:S(2)}, u32[]{:S(2)}) collective-permute-start(f32[1024,3,3,128]{3,0,2,1:T(8,128)} %add.91), channel_id=1, source_target_pairs={{0,128},{8,136},{16,144},{24,152},{32,160},{40,168},{48,176},{56,1... | collective-permute-start | bytes 14155784 | tf_op jit(solution)/shard_map/ppermute | solution.py:63
Sparse Core Ops, SparseCore 0:
  9.8 42.4 all-gather.1
  227.2 57.9 reduce-scatter.1
